TPU v7x, 32 devices: a whole 2x2x4 slice. The times are simulated.
32 devices in a mesh: member: 8 (over z, x), cell: 4 (over y, core).
Axes of the slice: x: 2, y: 2, z: 4, core: 2. Of those that a mesh axis runs over, the one named last changes fastest.
Arguments:
- latent: bfloat16 [8, 6144, 1024], P('member', 'cell'), may hold values from -6 to 6
- w_in: bfloat16 [1024, 1024], replicated, may hold values from -0.1875 to 0.1875
- w_out: bfloat16 [1024, 96], replicated, may hold values from -0.1875 to 0.1875
- target: bfloat16 [96, 6144], P(None, 'cell'), may hold values from -6 to 6
- cell_mask: int32 [6144], P('cell'), may hold values 0 or 1
Outputs:
- grad_w_in: float32 [1024, 1024], P(('member', 'cell'))
- grad_w_out: float32 [1024, 96], P(('member', 'cell'))
All inputs are finite; a program needn't handle non-finite values. No bound on the sum of `cell_mask` on one device may be relied on, other than what follows from the above.
Results may differ from a plain program's by a relative error of at most 0.0055.
Values may be sent and summed in bfloat16 or wider, within the bound.
A program may use at most 64 MiB of HBM per device.

v0:
```python
import jax
import jax.numpy as jnp
from jax import lax
from jax.sharding import PartitionSpec as P


def kernel_fn(diff):
    return diff / jnp.sqrt(1.0 + diff * diff)


def silu_slope(pre):
    gate = jax.nn.sigmoid(pre)
    return gate * (1.0 + pre * (1.0 - gate))


def per_device(latent, w_in, w_out, target, cell_mask):
    members = lax.axis_size("member")
    cell_count = lax.axis_size("cell")
    own_latent = latent[0]
    cells_here = own_latent.shape[0]
    scale = 1.0 / jnp.sqrt(jnp.float32(cells_here * cell_count))
    pre = jnp.dot(own_latent, w_in, preferred_element_type=jnp.float32)
    hidden = jax.nn.silu(pre).astype(jnp.bfloat16)
    fields = lax.dot_general(
        w_out, hidden, (((0,), (1,)), ((), ())), preferred_element_type=jnp.float32
    ).astype(jnp.bfloat16)
    wide = fields.astype(jnp.float32)
    pair = jnp.sum(
        kernel_fn(
            wide[None]
            - lax.all_gather(fields[None], "member", axis=0, tiled=True).astype(jnp.float32)
        ),
        axis=0,
    )
    weight = cell_mask.astype(jnp.float32) * scale / members
    own_term = kernel_fn(wide - target.astype(jnp.float32))
    grad_fields = (weight[None] * (own_term - pair / members)).astype(jnp.bfloat16)
    back = lax.dot_general(
        grad_fields, w_out, (((0,), (1,)), ((), ())), preferred_element_type=jnp.float32
    )
    grad_pre = (back * silu_slope(pre)).astype(jnp.bfloat16)
    width = w_in.shape[1]
    grad_in = lax.dot_general(
        own_latent, grad_pre, (((0,), (0,)), ((), ())), preferred_element_type=jnp.float32
    )
    grad_out = lax.dot_general(
        hidden, grad_fields, (((0,), (1,)), ((), ())), preferred_element_type=jnp.float32
    )
    owned = lax.psum_scatter(
        jnp.concatenate([grad_in, grad_out], axis=1),
        ("member", "cell"),
        scatter_dimension=0,
        tiled=True,
    )
    return (owned[:, :width], owned[:, width:])


def solution(mesh):
    in_specs = (P("member", "cell", None), P(), P(), P(None, "cell"), P("cell"))
    out_specs = (P(("member", "cell"), None), P(("member", "cell"), None))
    return jax.shard_map(
        per_device, mesh=mesh, in_specs=in_specs, out_specs=out_specs, check_vma=False
    )
```

profile of v0, /device:TPU:0, one launch (start us, length us, event | category | flops | bytes accessed | tf_op | source)
XLA Modules:
  0.0 217.5 jit_solution(14600535981441059085)
XLA Ops:
  7.2 0.0 copy-start
  7.2 0.0 all-gather.3.cloned.1.call-start
  7.2 1.8 copy-done
  9.1 7.5 %multiply_convert_fusion.1 = (bf16[1536,1024]{1,0:T(8,128)(2,1)S(1)}, f32[1536,1024]{1,0:T(8,128)}) fusion(bf16[1024,1024]{1,0:T(8,128)(2,1)} %param.6, bf16[1,1536,1024]{2,1,0:T(8,128)(2,1)S(1)} %copy-done), kind=kOutput, calls=%fused_computation.1 | convolution fusion | flops 3229089792 | bytes 14680064 | tf_op jit(solution)/shard_map/dot_general | solution.py:22
  16.6 1.7 copy-done.1
  18.3 0.0 copy-done.5
  18.3 2.0 fusion.14
  20.3 0.0 all-gather.3.cloned.1.call-update
  20.4 0.0 reduce-scatter.4.cloned.1.call-start
  20.4 0.0 copy-done.6
  20.4 54.6 %all-gather.3.cloned.1.call-done = bf16[768,1536]{1,0:T(8,128)(2,1)} async-done(((bf16[96,1536]{1,0:T(8,128)(2,1)}), bf16[768,1536]{1,0:T(8,128)(2,1)}) %all-gather.3.cloned.1.call-update) | async-done | bytes 2359312 | tf_op jit(solution)/shard_map/all_gather | solution.py:31
  75.1 3.1 %fusion.4 = f32[96,1536]{1,0:T(8,128)S(1)} fusion(bf16[8,96,1536]{2,1,0:T(8,128)(2,1)} %bitcast.23, f32[96,1536]{1,0:T(8,128)} %get-tuple-element.8), kind=kLoop, calls=%fused_computation.8 | loop fusion | flops 6930432 | bytes 3538944 | tf_op jit(solution)/shard_map/reduce_sum | solution.py:28
  78.1 1.2 multiply_convert_fusion.2
  79.3 0.0 copy-done.2
  79.3 0.0 copy-start.3
  79.3 0.6 fusion.15
  80.0 0.1 copy-done.3
  80.0 10.6 %fusion.10 = f32[1024,1024]{0,1:T(8,128)} fusion(bf16[1,1536,1024]{2,1,0:T(8,128)(2,1)S(1)} %copy-done, f32[1536,1024]{1,0:T(8,128)} %get-tuple-element.7, bf16[96,1536]{1,0:T(8,128)(2,1)} %copy-done.3, bf16[1024,96]{0,1:T(8,128)(2,1)} %param.7), kind=kOutput, calls=%fused_computation.16 | convolution fusion | flops 3537371136 | bytes 14123008 | tf_op jit(solution)/shard_map/dot_general | solution.py:43
  90.7 5.0 %pad_maximum_fusion = f32[1024,1120]{0,1:T(8,128)} fusion(f32[1024,96]{0,1:T(8,128)S(1)} %fusion.15, f32[1024,1024]{0,1:T(8,128)} %fusion.10), kind=kLoop, calls=%fused_computation.9 | loop fusion | flops 1146880 | bytes 9175040 | tf_op jit(solution)/shard_map/concatenate | solution.py:50
  95.7 5.9 %copy.11 = f32[1024,1120]{1,0:T(8,128)} copy(f32[1024,1120]{0,1:T(8,128)} %pad_maximum_fusion) | data formatting | bytes 9175040
  101.6 0.0 reduce-scatter.4.cloned.1.call-update
  101.6 106.2 %reduce-scatter.4.cloned.1.call-done = f32[32,1120]{1,0:T(8,128)} async-done(((f32[1024,1120]{1,0:T(8,128)}), f32[32,1120]{1,0:T(8,128)}) %reduce-scatter.4.cloned.1.call-update) | async-done | bytes 143376
  207.8 1.6 slice.8
  209.3 1.3 slice.9
  (7 shorter events, 0.0 us)
Async XLA Ops:
  7.2 1.9 copy-start
  7.2 67.9 %all-gather.3.cloned.1.call-start = ((), (), s32[]{:S(2)}) async-start(), calls=%async_computation.1 | async-start | bytes 2654208 | tf_op jit(solution)/shard_map/all_gather | solution.py:31
  9.1 9.2 %copy-start.5 = (bf16[1024,96]{0,1:T(8,128)(2,1)S(1)}, bf16[1024,96]{0,1:T(8,128)(2,1)}, u32[]{:S(2)}) copy-start(bf16[1024,96]{0,1:T(8,128)(2,1)} %param.7) | copy-start | bytes 589828
  16.6 1.7 copy-start.1
  16.6 3.8 %copy-start.6 = (s32[1536]{0:T(1024)S(1)}, s32[1536]{0:T(1024)}, u32[]{:S(2)}) copy-start(s32[1536]{0:T(1024)} %param.9) | copy-start | bytes 18436
  18.3 59.8 %copy-start.4 = (bf16[96,1536]{1,0:T(8,128)(2,1)S(1)}, bf16[96,1536]{1,0:T(8,128)(2,1)}, u32[]{:S(2)}) copy-start(bf16[96,1536]{1,0:T(8,128)(2,1)} %param.8) | copy-start | bytes 884740
  20.4 187.4 %reduce-scatter.4.cloned.1.call-start = ((), (), s32[]{:S(2)}) async-start(), calls=%async_computation.2 | async-start | bytes 4866048
  75.0 4.3 %copy-start.2 = (bf16[1536,1024]{1,0:T(8,128)(2,1)S(1)}, bf16[1536,1024]{1,0:T(8,128)(2,1)}, u32[]{:S(2)}) copy-start(bf16[1536,1024]{1,0:T(8,128)(2,1)} %copy-done.1) | copy-start | bytes 9437188
  79.3 0.7 copy-start.3
Sparse Core Ops, SparseCore 0:
  20.5 54.5 all-gather.2
  101.7 105.9 reduce-scatter.3
where the time goes:
time: 218 us
  waiting for transfers between devices  161 us (74%)
  matrix products  20.8 us (10%)
  between operations  14.1 us (6%)
  local copies, waits for them, and re-layouts  12.5 us (6%)
  other arithmetic  9.23 us (4%)
    unnamed x3, waiting for transfers between devices  106 us
    all_gather x1, waiting for transfers between devices, per_device(): lax.all_gather(fields[None], 'member', axis=0, tiled=True)  54.6 us
    dot_general x1, matrix products, per_device(): lax.dot_general(own_latent, grad_pre, (((0,), (0,)), ((), ())), preferred...  10.6 us
    unnamed x15, local copies, waits for them, and re-layouts  9.56 us
    dot_general x1, matrix products, per_device(): pre = jnp.dot(own_latent, w_in, preferred_element_type=jnp.float32)  7.54 us
    concatenate x1, other arithmetic, per_device(): jnp.concatenate([grad_in, grad_out], axis=1)  4.99 us
  transfers between devices with their start and end apart: 2, of which 2 were waited for; matrix products, arithmetic and copies ran while one was open for 0% of the time, Pallas kernels for 0%

commit v1 on v0

--- a/solution.py
+++ b/solution.py
@@ -28,7 +28,10 @@
     pair = jnp.sum(
         kernel_fn(
             wide[None]
-            - lax.all_gather(fields[None], "member", axis=0, tiled=True).astype(jnp.float32)
+            - jnp.concatenate(
+                lax.all_to_all(jnp.stack([fields[None]] * lax.axis_size("member")), "member", 0, 0),
+                axis=0,
+            ).astype(jnp.float32)
         ),
         axis=0,
     )

time: 218 us -> 227 us (1.041)
  starting transfers between devices: 0.08 us -> 7.32 us
    all_gather x1 -> x0, waiting for transfers between devices: 54.6 us -> none  [per_device(): lax.all_gather(fields[None], 'member', axis=0, tiled=True)]
    all_to_all x0 -> x1, waiting for transfers between devices: none -> 53.9 us  [per_device(): lax.all_to_all(jnp.stack([fields[None]] * lax.axis_size('member')), 'memb...]
    all_to_all x0 -> x1, starting transfers between devices: none -> 7.28 us  [per_device(): lax.all_to_all(jnp.stack([fields[None]] * lax.axis_size('member')), 'memb...]
    unnamed x3 -> x2, waiting for transfers between devices: 106 us -> 107 us
    unnamed x15 -> x13, local copies, waits for them, and re-layouts: 9.56 us -> 9.61 us
where the time goes in v1:
time: 227 us; the launch traced here: 226 us
  waiting for transfers between devices  161 us (71%)
  matrix products  20.7 us (9%)
  local copies, waits for them, and re-layouts  14.2 us (6%)
  between operations  14.1 us (6%)
  other arithmetic  9.24 us (4%)
  starting transfers between devices  7.32 us (3%)
    unnamed x2, waiting for transfers between devices  107 us
    all_to_all x1, waiting for transfers between devices, per_device(): lax.all_to_all(jnp.stack([fields[None]] * lax.axis_size('member')), 'memb...  53.9 us
    dot_general x1, matrix products, per_device(): lax.dot_general(own_latent, grad_pre, (((0,), (0,)), ((), ())), preferred...  10.7 us
    unnamed x13, local copies, waits for them, and re-layouts  9.61 us
    dot_general x1, matrix products, per_device(): pre = jnp.dot(own_latent, w_in, preferred_element_type=jnp.float32)  7.49 us
    all_to_all x1, starting transfers between devices, per_device(): lax.all_to_all(jnp.stack([fields[None]] * lax.axis_size('member')), 'memb...  7.28 us
    concatenate x1, other arithmetic, per_device(): jnp.concatenate([grad_in, grad_out], axis=1)  5 us
  transfers between devices with their start and end apart: 2, of which 2 were waited for; matrix products, arithmetic and copies ran while one was open for 0% of the time, Pallas kernels for 0%

profile of v1, /device:TPU:0, one launch (start us, length us, event | category | flops | bytes accessed | tf_op | source)
XLA Modules:
  0.0 226.4 jit_solution(4223334116127603561)
XLA Ops:
  7.2 0.0 copy-start
  7.2 0.0 copy-start.4
  7.2 1.9 copy-done
  9.1 7.5 %multiply_convert_fusion.1 = (bf16[1536,1024]{1,0:T(8,128)(2,1)S(1)}, f32[1536,1024]{1,0:T(8,128)}) fusion(bf16[1024,1024]{1,0:T(8,128)(2,1)} %param.6, bf16[1,1536,1024]{2,1,0:T(8,128)(2,1)S(1)} %copy-done), kind=kOutput, calls=%fused_computation.1 | convolution fusion | flops 3229089792 | bytes 14680064 | tf_op jit(solution)/shard_map/dot_general | solution.py:22
  16.5 1.7 copy-done.1
  18.2 0.0 copy-done.4
  18.2 1.9 fusion.14
  20.2 1.7 stack.3
  21.8 7.3 %all-to-all-start = ((bf16[8,1,96,1536]{3,2,1,0:T(8,128)(2,1)}), bf16[8,1,96,1536]{3,2,1,0:T(8,128)(2,1)}, u32[]{:S(2)}, u32[]{:S(2)}) async-start(bf16[8,1,96,1536]{3,2,1,0:T(8,128)(2,1)} %stack.3), calls=%async_computation | async-start | bytes 4718592 | tf_op jit(solution)/shard_map/all_to_all | solution.py:32
  29.1 0.0 reduce-scatter.4.cloned.1.call-start
  29.2 53.9 %all-to-all-done = bf16[8,1,96,1536]{3,2,1,0:T(8,128)(2,1)} async-done(((bf16[8,1,96,1536]{3,2,1,0:T(8,128)(2,1)}), bf16[8,1,96,1536]{3,2,1,0:T(8,128)(2,1)}, u32[]{:S(2)}, u32[]{:S(2)}) %all-to-all-start) | async-done | bytes 2359328 | tf_op jit(solution)/shard_map/all_to_all | solution.py:32
  83.1 3.1 %fusion.4 = f32[96,1536]{1,0:T(8,128)S(1)} fusion(bf16[8,1,96,1536]{3,2,1,0:T(8,128)(2,1)} %all-to-all-done, f32[96,1536]{1,0:T(8,128)} %get-tuple-element.8), kind=kLoop, calls=%fused_computation.8 | loop fusion | flops 6930432 | bytes 3538944 | tf_op jit(solution)/shard_map/reduce_sum | solution.py:28
  86.2 1.2 multiply_convert_fusion.2
  87.3 0.0 copy-done.2
  87.3 0.0 copy-start.3
  87.4 0.6 fusion.15
  88.0 0.1 copy-done.3
  88.1 10.7 %fusion.10 = f32[1024,1024]{0,1:T(8,128)} fusion(bf16[1,1536,1024]{2,1,0:T(8,128)(2,1)S(1)} %copy-done, f32[1536,1024]{1,0:T(8,128)} %get-tuple-element.7, bf16[96,1536]{1,0:T(8,128)(2,1)} %copy-done.3, bf16[1024,96]{0,1:T(8,128)(2,1)} %param.7), kind=kOutput, calls=%fused_computation.16 | convolution fusion | flops 3537371136 | bytes 14123008 | tf_op jit(solution)/shard_map/dot_general | solution.py:46
  98.7 5.0 %pad_maximum_fusion = f32[1024,1120]{0,1:T(8,128)} fusion(f32[1024,96]{0,1:T(8,128)S(1)} %fusion.15, f32[1024,1024]{0,1:T(8,128)} %fusion.10), kind=kLoop, calls=%fused_computation.9 | loop fusion | flops 1146880 | bytes 9175040 | tf_op jit(solution)/shard_map/concatenate | solution.py:53
  103.7 6.0 %copy.11 = f32[1024,1120]{1,0:T(8,128)} copy(f32[1024,1120]{0,1:T(8,128)} %pad_maximum_fusion) | data formatting | bytes 9175040
  109.7 0.0 reduce-scatter.4.cloned.1.call-update
  109.7 106.9 %reduce-scatter.4.cloned.1.call-done = f32[32,1120]{1,0:T(8,128)} async-done(((f32[1024,1120]{1,0:T(8,128)}), f32[32,1120]{1,0:T(8,128)}) %reduce-scatter.4.cloned.1.call-update) | async-done | bytes 143376
  216.6 1.6 slice.8
  218.2 1.3 slice.9
  (5 shorter events, 0.0 us)
Async XLA Ops:
  7.2 1.9 copy-start
  7.2 11.1 %copy-start.4 = (bf16[1024,96]{0,1:T(8,128)(2,1)S(1)}, bf16[1024,96]{0,1:T(8,128)(2,1)}, u32[]{:S(2)}) copy-start(bf16[1024,96]{0,1:T(8,128)(2,1)} %param.7) | copy-start | bytes 589828
  16.5 1.7 copy-start.1
  20.2 9.0 %copy-start.5 = (s32[1536]{0:T(1024)S(1)}, s32[1536]{0:T(1024)}, u32[]{:S(2)}) copy-start(s32[1536]{0:T(1024)} %param.9) | copy-start | bytes 18436
  21.8 61.2 %all-to-all-start = ((bf16[8,1,96,1536]{3,2,1,0:T(8,128)(2,1)}), bf16[8,1,96,1536]{3,2,1,0:T(8,128)(2,1)}, u32[]{:S(2)}, u32[]{:S(2)}) async-start(bf16[8,1,96,1536]{3,2,1,0:T(8,128)(2,1)} %stack.3), calls=%async_computation | async-start | bytes 4718592 | tf_op jit(solution)/shard_map/all_to_all | solution.py:32
  29.1 187.5 %reduce-scatter.4.cloned.1.call-start = ((), (), s32[]{:S(2)}) async-start(), calls=%async_computation.2 | async-start | bytes 4866048
  83.1 4.2 %copy-start.2 = (bf16[1536,1024]{1,0:T(8,128)(2,1)S(1)}, bf16[1536,1024]{1,0:T(8,128)(2,1)}, u32[]{:S(2)}) copy-start(bf16[1536,1024]{1,0:T(8,128)(2,1)} %copy-done.1) | copy-start | bytes 9437188
  87.3 0.7 copy-start.3
Sparse Core Ops, SparseCore 0:
  109.8 106.7 reduce-scatter.3
